TPU v7x, 32 devices: a whole 2x2x4 slice. The times are simulated.
32 devices in a mesh: seq: 8 (over z, y), pat: 4 (over x, core).
Axes of the slice: x: 2, y: 2, z: 4, core: 2. Of those that a mesh axis runs over, the one named last changes fastest.
Arguments:
- queries: bfloat16 [4, 2048, 2048], P('pat', 'seq'), may hold values from -6 to 6
- key_rows: bfloat16 [4, 2048, 2048], P('pat', 'seq'), may hold values from -6 to 6
- value_rows: bfloat16 [4, 2048, 2048], P('pat', 'seq'), may hold values from -6 to 6
- out_weight: bfloat16 [2048, 2048], P('pat'), may hold values from -0.125 to 0.125
- grad_out: bfloat16 [4, 2048, 2048], P('pat', 'seq'), may hold values from -6 to 6
- visit_mask: int32 [4, 8, 2, 2], P('pat', 'seq'), may hold values 0 or 1
- lengths: int32 [4], P('pat'), may hold values from 256 to 2048, as said below
Outputs:
- mixed: bfloat16 [4, 2048, 2048], P('pat', 'seq')
- query_grad: bfloat16 [4, 2048, 2048], P('pat', 'seq')
- key_grad: bfloat16 [4, 2048, 2048], P('pat', 'seq')
- value_grad: bfloat16 [4, 2048, 2048], P('pat', 'seq')
- weight_grad: float32 [2048, 2048], P('pat', 'seq')
Inputs may be any that keep to these rules, and one draw needn't show every extreme that they name: `lengths`: one patient's record fills all 2048 positions in every draw.
All inputs are finite; a program needn't handle non-finite values. No bound on the sum of `visit_mask` on one device may be relied on, other than what follows from the above.
Results may differ from a plain program's by a relative error of at most 0.013.
Values may be sent and summed in bfloat16 or wider, within the bound.
A program may use at most 384 MiB of HBM per device.

v0:
```python
import math

import jax
import jax.numpy as jnp
from jax import lax
from jax.experimental import pallas as pl
from jax.experimental.pallas import tpu as pltpu
from jax.sharding import PartitionSpec as P

HD = 128
NCH = 4
MESH = pl.DeviceIdType.MESH
F32 = jnp.float32
BF = jnp.bfloat16


def dot(a, b, ca, cb):
    return lax.dot_general(a, b, (((ca,), (cb,)), ((), ())), preferred_element_type=F32)


def make_kernel(n, np_, rows, width, nb, grad_scale):
    heads = width // HD
    per = heads // np_
    blk = per * HD
    piece = width // n
    m = n // 2
    half_rows = heads * HD // 2
    zrows = half_rows // m
    wrows = blk // NCH

    def kernel(
        q, k, v, go, w, vm, ln,
        mixed, dq, dk, dv, wg,
        w_all, go_all, att, attc, att_t, sc, allowed, g, dk0, dv0,
        st, sb, rv, sa, box1, pair1, zbox1, px1, pz1, pd1,
        box2, pair2, zbox2, px2, pz2, pd2, part, pbox, psum, zpart,
        lsem, ps, pr, ys, yr, zs, zr,
    ):
        me = lax.axis_index("pat")
        si = lax.axis_index("seq")
        sib = me + 1 - 2 * (me % 2)
        xp = (me + 2) % np_
        diag = (sib + 2) % np_
        yi = si % 2
        zi = si // 2
        yo = 1 - yi
        partner = si + 1 - 2 * yi

        def zpeer(d):
            return ((zi + d) % m) * 2 + yi

        barrier = pltpu.get_barrier_semaphore()
        for peer in (sib, xp, diag):
            pl.semaphore_signal(barrier, inc=1, device_id={"pat": peer}, device_id_type=MESH)
        for peer in [partner] + [zpeer(d) for d in range(1, m)]:
            pl.semaphore_signal(barrier, inc=1, device_id={"seq": peer}, device_id_type=MESH)
        pl.semaphore_wait(barrier, 3 + m)

        def pat_copy(src, dst, i, peer):
            return pltpu.make_async_remote_copy(
                src_ref=src, dst_ref=dst, send_sem=ps.at[i], recv_sem=pr.at[i],
                device_id={"pat": peer}, device_id_type=MESH,
            )

        def y_copy(src, dst, i):
            return pltpu.make_async_remote_copy(
                src_ref=src, dst_ref=dst, send_sem=ys.at[i], recv_sem=yr.at[i],
                device_id={"seq": partner}, device_id_type=MESH,
            )

        def z_copy(src, dst, i, d):
            return pltpu.make_async_remote_copy(
                src_ref=src, dst_ref=dst, send_sem=zs.at[i, d], recv_sem=zr.at[i, d],
                device_id={"seq": zpeer(d)}, device_id_type=MESH,
            )

        def wsl(c):
            return pl.ds(pl.multiple_of(c * wrows, wrows), wrows)

        local_w = pltpu.make_async_copy(w, w_all.at[me], lsem.at[0])
        local_go = pltpu.make_async_copy(go, go_all.at[me], lsem.at[1])
        go_sib = pat_copy(go, go_all.at[me], 0, sib)
        go_xp = pat_copy(go, go_all.at[me], 1, xp)
        go_relay = pat_copy(go_all.at[xp], go_all.at[xp], 2, sib)
        w_sib = pat_copy(w, w_all.at[me], 3, sib)
        zb = zi % 2
        zpair = (zi + 1 - 2 * zb) * 2 + yi
        spots = [
            wsl(yi * 2 + zb), wsl(yi * 2 + 1 - zb), wsl(yo * 2 + zb), wsl(yo * 2 + 1 - zb)
        ]
        near = [w_all.at[xp, spot] for spot in spots]
        w_xp = pat_copy(w.at[spots[0]], w_all.at[me, spots[0]], 4, xp)
        w_z = pltpu.make_async_remote_copy(
            src_ref=near[0], dst_ref=near[0], send_sem=lsem.at[2], recv_sem=lsem.at[3],
            device_id={"seq": zpair}, device_id_type=MESH,
        )
        w_y = [y_copy(near[c], near[c], 4 + m + c) for c in range(2)]
        w_relay = [pat_copy(near[c], near[c], 5 + c, sib) for c in range(NCH)]
        first = 5 + NCH
        att_out = [
            pat_copy(att.at[peer], attc.at[me], first + i, peer)
            for i, peer in enumerate((sib, xp, diag))
        ]
        w_xp.start()
        go_xp.start()
        w_sib.start()
        go_sib.start()
        local_w.start()
        local_go.start()

        pos_c = si * rows + lax.broadcasted_iota(jnp.int32, (rows, 1), 0)
        pos_r = si * rows + lax.broadcasted_iota(jnp.int32, (1, rows), 1)
        live = jnp.where(pos_c < ln[0], 1.0, 0.0).astype(F32)
        live_r = jnp.where(pos_r < ln[0], 1.0, 0.0).astype(F32)
        live_h = live.astype(BF)
        scale = live * lax.rsqrt((pos_c + 1).astype(F32)) / math.sqrt(HD)

        def lanes(pb, i, size=HD):
            return pl.ds(pl.multiple_of(pb * blk + i * HD, HD), size)

        @pl.loop(0, np_)
        def _(pb):
            for i in range(per):
                ls = lanes(pb, i)
                st[ls, :] = dot(k[:, ls] * live_h, v[:, ls], 0, 0).astype(BF)

        def half(i):
            return pl.ds(pl.multiple_of(i * half_rows, half_rows), half_rows)

        def z_of(i):
            return pl.ds(pl.multiple_of(i * zrows, zrows), zrows)

        def wait(copies):
            for copy in copies:
                copy.wait()

        class Scan:
            def __init__(self, own, dst, box, pair, zbox, px, pz, pd, base, forward):
                self.own, self.dst, self.box, self.pair = own, dst, box, pair
                self.zbox, self.px, self.pz, self.pd = zbox, px, pz, pd
                self.forward = forward
                self.order = range(m) if forward else range(m - 1, -1, -1)
                self.a = y_copy(own.at[half(yo)], box, base)
                self.b = [
                    z_copy(pair.at[z_of((zi + d) % m)], zbox.at[zi], base, d) for d in range(1, m)
                ]
                self.c = [
                    z_copy(px.at[(zi + d) % m], pz.at[z_of(zi)], base + 1, d) for d in range(1, m)
                ]
                self.d = y_copy(pd, dst.at[half(yi)], base + 1)

            def run_a(self):
                self.a.start()

            def run_b(self):
                self.a.wait()
                both = self.own[half(yi), :].astype(F32) + self.box[...].astype(F32)
                self.pair[...] = both.astype(BF)
                for copy in self.b:
                    copy.start()
                self.zbox[zi] = self.pair[z_of(zi), :]

            def run_c(self):
                wait(self.b)
                total = jnp.zeros((zrows, HD), F32)
                for s in self.order:
                    self.px[s] = total.astype(BF)
                    total = total + self.zbox[s].astype(F32)
                for copy in self.c:
                    copy.start()
                self.pz[z_of(zi), :] = self.px[zi]

            def run_d(self):
                wait(self.c)
                late = (yi if self.forward else yo).astype(F32)
                base = self.pz[...].astype(F32)
                give = base + (1.0 - late) * self.own[half(yi), :].astype(F32)
                self.pd[...] = give.astype(BF)
                self.d.start()
                keep = base + late * self.box[...].astype(F32)
                self.dst[half(yi), :] = keep.astype(BF)

        fwd = Scan(st, sb, box1, pair1, zbox1, px1, pz1, pd1, 0, True)
        bwd = Scan(rv, sa, box2, pair2, zbox2, px2, pz2, pd2, 2, False)
        fwd.run_a()

        row_i = lax.broadcasted_iota(jnp.int32, (rows, rows), 0)
        col_i = lax.broadcasted_iota(jnp.int32, (rows, rows), 1)
        rb, cb = row_i // (rows // nb), col_i // (rows // nb)
        keep = jnp.where(rb == cb, 1.0, 0.0).astype(F32)
        for i in range(nb):
            for j in range(i):
                on = jnp.where(vm[0, 0, i, j] == 1, 1.0, 0.0).astype(F32)
                keep = keep + jnp.where((rb == i) & (cb == j), on, 0.0)
        allowed[...] = jnp.where(row_i >= col_i, keep, 0.0) * live * live_r

        def grad_block(pb):
            @pl.loop(0, blk // 256)
            def _(c):
                at = pl.ds(pl.multiple_of(c * 256, 256), 256)
                ga = dot(go[...], w_all[pb, at, :], 1, 1).astype(BF)
                gg = (scale * ga.astype(F32)).astype(BF)
                g[:, pl.ds(pl.multiple_of(pb * blk + c * 256, HD), 256)] = gg
                for i in range(256 // HD):
                    ls = pl.ds(pl.multiple_of(pb * blk + c * 256 + i * HD, HD), HD)
                    rv[ls, :] = dot(q[:, ls], gg[:, i * HD : (i + 1) * HD], 0, 0).astype(BF)

        def grads(pb):
            for i in range(per):
                ls = lanes(pb, i)
                gh = g[:, ls]
                inner = (dot(gh, v[:, ls], 1, 1) * allowed[...]).astype(BF)
                dq[:, ls] = (dot(inner, k[:, ls], 1, 0) + dot(gh, sb[ls, :], 1, 1)).astype(BF)
                dk0[:, ls] = dot(inner, q[:, ls], 0, 0)
                dv0[:, ls] = dot(sc[pb * per + i], gh, 0, 0)

        fwd.run_b()

        @pl.loop(0, np_)
        def _(pb):
            for i in range(per):
                ls = lanes(pb, i)
                s = dot(q[:, ls], k[:, ls], 1, 1) * allowed[...]
                sc[pb * per + i] = s.astype(BF)

        local_w.wait()
        local_go.wait()
        fwd.run_c()
        w_xp.wait()
        w_z.start()
        w_y[0].start()
        w_relay[0].start()
        grad_block(me)
        w_sib.wait()
        grad_block(sib)
        fwd.run_d()
        w_z.wait()
        w_y[1].start()
        w_relay[1].start()
        fwd.d.wait()

        @pl.loop(0, np_)
        def _(pb):
            for i in range(per):
                ls = lanes(pb, i)
                inner = dot(sc[pb * per + i], v[:, ls], 1, 0) + dot(q[:, ls], sb[ls, :], 1, 0)
                att[pb, :, i * HD : (i + 1) * HD] = (scale * inner).astype(BF)

        for copy in att_out:
            copy.start()

        @pl.loop(0, 2)
        def _(i):
            grads(me + (sib - me) * i)

        for c in range(2):
            w_y[c].wait()
            w_relay[2 + c].start()
        go_xp.wait()
        go_relay.start()
        grad_block(xp)
        wait(w_relay)
        grad_block(diag)
        bwd.run_a()
        att_t[me] = att[me].T
        go_sib.wait()
        go_relay.wait()
        for copy, peer in zip(att_out, (sib, xp, diag)):
            copy.wait()
            att_t[peer] = attc[peer].T

        def product(cols):
            acc = dot(att_t[0], go_all[0, :, cols], 1, 0)
            for b in range(1, np_):
                acc = acc + dot(att_t[b], go_all[b, :, cols], 1, 0)
            return acc

        def cols_of(i):
            return pl.ds(pl.multiple_of(i * piece, HD), piece)

        y_out = [None] * (m + 1)
        if piece % HD:
            for j in range(width // 256):
                acc = product(slice(j * 256, (j + 1) * 256))
                for i in range(256 // piece):
                    part[j * (256 // piece) + i] = acc[:, i * piece : (i + 1) * piece].astype(BF)
        for d in range(1, m + 1):
            to = (zi + d) % m
            if piece % HD == 0:
                part[to * 2 + yo] = product(cols_of(to * 2 + yo)).astype(BF)
            y_out[d] = y_copy(part.at[to * 2 + yo], pbox.at[to], 3 + d)
            y_out[d].start()
        bwd.run_b()

        @pl.loop(0, 2)
        def _(i):
            grads(xp + (diag - xp) * i)

        bwd.run_c()
        z_out = []
        for d in range(1, m + 1):
            to = (zi + d) % m
            if piece % HD == 0:
                acc = product(cols_of(to * 2 + yi))
            else:
                acc = part[to * 2 + yi].astype(F32)
            y_out[d].wait()
            acc = acc + pbox[to].astype(F32)
            psum[to] = acc.astype(BF)
            if d < m:
                copy = z_copy(psum.at[to], zpart.at[zi], 4, d)
                copy.start()
                z_out.append(copy)
            else:
                zpart[zi] = psum[to]
        bwd.run_d()

        @pl.loop(0, width // 256)
        def _(j):
            cols = pl.ds(pl.multiple_of(j * 256, 256), 256)
            acc = dot(att[0], w_all[0, :, cols], 1, 0)
            for b in range(1, np_):
                acc = acc + dot(att[b], w_all[b, :, cols], 1, 0)
            mixed[:, cols] = acc.astype(BF)

        bwd.d.wait()

        @pl.loop(0, np_)
        def _(pb):
            for i in range(per):
                ls = lanes(pb, i)
                dk[:, ls] = (dk0[:, ls] + live * dot(v[:, ls], sa[ls, :], 1, 1)).astype(BF)
                dv[:, ls] = (dv0[:, ls] + live * dot(k[:, ls], sa[ls, :], 1, 0)).astype(BF)

        wait(z_out)
        total = zpart[0].astype(F32)
        for s in range(1, m):
            total = total + zpart[s].astype(F32)
        wg[...] = total * grad_scale

    vmem = pltpu.VMEM
    sems = pltpu.SemaphoreType.DMA
    state = vmem((heads * HD, HD), BF)
    half_state = vmem((half_rows, HD), BF)
    by_z = vmem((m, zrows, HD), BF)
    scan_boxes = [half_state, half_state, by_z, by_z, half_state, half_state]
    n_pat = 8 + NCH
    n_y = 6 + m
    scratch = [
        vmem((np_, blk, width), BF),
        vmem((np_, rows, width), BF),
        vmem((np_, rows, blk), BF),
        vmem((np_, rows, blk), BF),
        vmem((np_, blk, rows), BF),
        vmem((heads, rows, rows), BF),
        vmem((rows, rows), F32),
        vmem((rows, width), BF),
        vmem((rows, width), F32),
        vmem((rows, width), F32),
        state, state, state, state,
        *scan_boxes,
        *scan_boxes,
        vmem((n, blk, piece), BF),
        vmem((m, blk, piece), BF),
        vmem((m, blk, piece), BF),
        vmem((m, blk, piece), BF),
        sems((4,)),
        sems((n_pat,)), sems((n_pat,)),
        sems((n_y,)), sems((n_y,)),
        sems((5, m)), sems((5, m)),
    ]
    full = jax.ShapeDtypeStruct((rows, width), BF)
    whole = pl.BlockSpec(memory_space=pltpu.VMEM)
    scalar = pl.BlockSpec(memory_space=pltpu.SMEM)
    return pl.pallas_call(
        kernel,
        out_shape=(full, full, full, full, jax.ShapeDtypeStruct((blk, piece), F32)),
        in_specs=[whole] * 5 + [scalar] * 2,
        out_specs=(whole,) * 5,
        scratch_shapes=scratch,
        compiler_params=pltpu.CompilerParams(
            collective_id=0, has_side_effects=True, vmem_limit_bytes=60 * 1024 * 1024
        ),
    )


def solution(mesh):
    n, np_ = mesh.shape["seq"], mesh.shape["pat"]

    def on_device(queries, key_rows, value_rows, out_weight, grad_out, visit_mask, lengths):
        rows, width = queries.shape[1:]
        call = make_kernel(
            n, np_, rows, width, visit_mask.shape[-1], 1.0 / math.sqrt(np_ * n * rows)
        )
        mixed, dq, dk, dv, wg = call(
            queries[0], key_rows[0], value_rows[0], grad_out[0], out_weight, visit_mask, lengths
        )
        return mixed[None], dq[None], dk[None], dv[None], wg

    rows3 = P("pat", "seq", None)
    return jax.shard_map(
        on_device,
        mesh=mesh,
        in_specs=(rows3, rows3, rows3, P("pat", None), rows3, P("pat", "seq", None, None), P("pat")),
        out_specs=(rows3, rows3, rows3, rows3, P("pat", "seq")),
        check_vma=False,
    )
```

profile of v0, /device:TPU:24, one launch (start us, length us, event | category | flops | bytes accessed | tf_op | source)
XLA Modules:
  0.0 107.8 jit_solution(13200732134945864012)
XLA Ops:
  1.3 100.3 %shard_map.110 = (bf16[256,2048]{1,0:T(8,128)(2,1)}, bf16[256,2048]{1,0:T(8,128)(2,1)}, bf16[256,2048]{1,0:T(8,128)(2,1)}, bf16[256,2048]{1,0:T(8,128)(2,1)}, f32[512,256]{1,0:T(8,128)}) custom-call(bf16[256,2048]{1,0:T(8,128)(2,1)} %bitcast.12, bf16[256,2048]{1,0:T(8,128)(2,1)} %bitcast.13, bf16[256,2048]{1,0:T(8,128)(2,1)} %bitcast.14, ...), custom_call_target="tpu_custom_call" | custom-call | tf_op jit(solution)/shard_map/pallas_call | solution.py:395
  101.6 0.0 copy-start.2
  101.6 0.0 copy-start.1
  101.6 2.5 %copy.18 = bf16[1,256,2048]{2,1,0:T(8,128)(2,1)} copy(bf16[1,256,2048]{2,1,0:T(8,128)(2,1)} %bitcast.11) | data formatting | bytes 2097152
  104.0 0.0 copy-done.2
  104.1 0.0 copy-start
  104.1 1.0 copy.19
  105.0 0.0 copy-done.1
  105.0 0.0 copy-start.3
  105.0 1.0 copy.20
  106.0 0.0 copy-done
  106.0 1.0 copy.21
  107.0 0.0 copy-done.3
  107.0 0.8 copy.22
Async XLA Ops:
  101.6 2.5 %copy-start.2 = (bf16[256,2048]{1,0:T(8,128)(2,1)S(1)}, bf16[256,2048]{1,0:T(8,128)(2,1)}, u32[]{:S(2)}) copy-start(bf16[256,2048]{1,0:T(8,128)(2,1)} %get-tuple-element.11) | copy-start | bytes 3145732
  101.6 3.4 %copy-start.1 = (bf16[256,2048]{1,0:T(8,128)(2,1)S(1)}, bf16[256,2048]{1,0:T(8,128)(2,1)}, u32[]{:S(2)}) copy-start(bf16[256,2048]{1,0:T(8,128)(2,1)} %get-tuple-element.12) | copy-start | bytes 3145732
  104.1 1.9 %copy-start = (bf16[256,2048]{1,0:T(8,128)(2,1)S(1)}, bf16[256,2048]{1,0:T(8,128)(2,1)}, u32[]{:S(2)}) copy-start(bf16[256,2048]{1,0:T(8,128)(2,1)} %get-tuple-element.13) | copy-start | bytes 3145732
  105.0 1.9 %copy-start.3 = (f32[512,256]{1,0:T(8,128)S(1)}, f32[512,256]{1,0:T(8,128)}, u32[]{:S(2)}) copy-start(f32[512,256]{1,0:T(8,128)} %get-tuple-element.24) | copy-start | bytes 1572868
where the time goes:
time: 108 us
  Pallas kernels  100 us (93%)
  local copies, waits for them, and re-layouts  6.17 us (6%)
  between operations  1.31 us (1%)
    pallas_call x1, Pallas kernels, on_device(): call(queries[0], key_rows[0], value_rows[0], grad_out[0], out_weight, vis...  100 us
    unnamed x13, local copies, waits for them, and re-layouts  6.17 us

commit v1 on v0

v1 whole, which is shorter than its diff:
```python
import math

import jax
import jax.numpy as jnp
from jax import lax
from jax.experimental import pallas as pl
from jax.experimental.pallas import tpu as pltpu
from jax.sharding import PartitionSpec as P

HD = 128
MESH = pl.DeviceIdType.MESH
F32 = jnp.float32
BF = jnp.bfloat16


def dot(a, b, ca, cb):
    return lax.dot_general(a, b, (((ca,), (cb,)), ((), ())), preferred_element_type=F32)


def make_kernel(n, np_, rows, width, nb, grad_scale):
    heads = width // HD
    per = heads // np_
    blk = per * HD
    piece = width // n
    m = n // 2
    half_rows = blk // 2
    zrows = half_rows // m
    wrows = blk // 8
    n_go = m if piece % HD == 0 else 1
    n_scan_y = 4 * np_

    def kernel(
        q, k, v, go, w, vm, ln,
        mixed, dq, dk, dv, wg,
        w_all, go_all, att, attc, att_t, sc, allowed, g, dk0, dv0,
        st, sb, rv, sa, box1, pair1, zbox1, px1, pz1, pd1,
        box2, pair2, zbox2, px2, pz2, pd2, part, pbox, psum, zpart,
        lsem, ps, pr, ys, yr, zs, zr,
    ):
        me = lax.axis_index("pat")
        si = lax.axis_index("seq")
        sib = me + 1 - 2 * (me % 2)
        xp = (me + 2) % np_
        diag = (sib + 2) % np_
        yi = si % 2
        zi = si // 2
        yo = 1 - yi
        partner = si + 1 - 2 * yi

        def zpeer(d):
            return ((zi + d) % m) * 2 + yi

        barrier = pltpu.get_barrier_semaphore()
        for peer in (sib, xp, diag):
            pl.semaphore_signal(barrier, inc=1, device_id={"pat": peer}, device_id_type=MESH)
        for peer in [partner] + [zpeer(d) for d in range(1, m)]:
            pl.semaphore_signal(barrier, inc=1, device_id={"seq": peer}, device_id_type=MESH)
        pl.semaphore_wait(barrier, 3 + m)

        def pat_copy(src, dst, i, peer):
            return pltpu.make_async_remote_copy(
                src_ref=src, dst_ref=dst, send_sem=ps.at[i], recv_sem=pr.at[i],
                device_id={"pat": peer}, device_id_type=MESH,
            )

        def y_copy(src, dst, i):
            return pltpu.make_async_remote_copy(
                src_ref=src, dst_ref=dst, send_sem=ys.at[i], recv_sem=yr.at[i],
                device_id={"seq": partner}, device_id_type=MESH,
            )

        def z_copy(src, dst, i, d):
            return pltpu.make_async_remote_copy(
                src_ref=src, dst_ref=dst, send_sem=zs.at[i, d], recv_sem=zr.at[i, d],
                device_id={"seq": zpeer(d)}, device_id_type=MESH,
            )

        local_w = pltpu.make_async_copy(w, w_all.at[me], lsem.at[0])
        local_go = pltpu.make_async_copy(go, go_all.at[me], lsem.at[1])
        w_sib = pat_copy(w, w_all.at[me], 0, sib)
        go_sib = pat_copy(go, go_all.at[me], 1, sib)
        att_out = [
            pat_copy(att.at[peer], attc.at[me], 2 + i, peer) for i, peer in enumerate((xp, diag, sib))
        ]

        def go_cols(d):
            if n_go == 1:
                return slice(None)
            return pl.ds(pl.multiple_of(((zi + d + 1) % m) * 2 * piece, HD), 2 * piece)

        go_x = [
            pat_copy(go.at[:, go_cols(d)], go_all.at[me, :, go_cols(d)], 5 + d, xp)
            for d in range(n_go)
        ]
        go_relay = [
            pat_copy(go_all.at[xp, :, go_cols(d)], go_all.at[xp, :, go_cols(d)], 5 + n_go + d, sib)
            for d in range(n_go)
        ]
        zb = zi % 2
        zpair = (zi + 1 - 2 * zb) * 2 + yi
        base_w = 5 + 2 * n_go

        def unit(y, z, h):
            at = ((y * 2 + z) * 2 + h) * wrows
            return pl.ds(pl.multiple_of(at, wrows), wrows)

        def zpair_copy(src, i):
            return pltpu.make_async_remote_copy(
                src_ref=src, dst_ref=src, send_sem=lsem.at[2 + i], recv_sem=lsem.at[5 + i],
                device_id={"seq": zpair}, device_id_type=MESH,
            )

        spots = [
            unit(yi, zb, 0), unit(yi, zb, 1), unit(yi, 1 - zb, 0), unit(yi, 1 - zb, 1),
            unit(yo, zb, 0), unit(yo, zb, 1), unit(yo, 1 - zb, 0), unit(yo, 1 - zb, 1),
        ]
        near = [w_all.at[xp, spot] for spot in spots]
        w_x = [pat_copy(w.at[spots[i]], w_all.at[me, spots[i]], base_w + i, xp) for i in range(2)]
        w_relay = [pat_copy(near[c], near[c], base_w + 2 + c, sib) for c in range(8)]
        w_z = [zpair_copy(near[c], i) for i, c in enumerate((0, 1, 5))]
        w_y = [y_copy(near[c], near[c], n_scan_y + i) for i, c in enumerate((0, 1, 2))]

        w_x[0].start()
        w_x[1].start()
        go_x[0].start()
        w_sib.start()
        go_sib.start()
        local_w.start()
        local_go.start()

        pos_c = si * rows + lax.broadcasted_iota(jnp.int32, (rows, 1), 0)
        pos_r = si * rows + lax.broadcasted_iota(jnp.int32, (1, rows), 1)
        live = jnp.where(pos_c < ln[0], 1.0, 0.0).astype(F32)
        live_r = jnp.where(pos_r < ln[0], 1.0, 0.0).astype(F32)
        live_h = live.astype(BF)
        scale = live * lax.rsqrt((pos_c + 1).astype(F32)) / math.sqrt(HD)

        def lanes(pb, i, size=HD):
            return pl.ds(pl.multiple_of(pb * blk + i * HD, HD), size)

        def half(pb, y):
            return pl.ds(pl.multiple_of(pb * blk + y * half_rows, half_rows), half_rows)

        def z_of(i):
            return pl.ds(pl.multiple_of(i * zrows, zrows), zrows)

        def wait(copies):
            for copy in copies:
                copy.wait()

        class Scan:
            def __init__(self, own, dst, bufs, g, pb, base, forward):
                self.own, self.dst, self.pb = own, dst, pb
                self.box, self.pair, self.zbox, self.px, self.pz, self.pd = [b.at[g] for b in bufs]
                self.forward = forward
                self.order = range(m) if forward else range(m - 1, -1, -1)
                self.a = y_copy(own.at[half(pb, yo)], self.box, base)
                self.b = [
                    z_copy(self.pair.at[z_of((zi + d) % m)], self.zbox.at[zi], base, d)
                    for d in range(1, m)
                ]
                self.c = [
                    z_copy(self.px.at[(zi + d) % m], self.pz.at[z_of(zi)], base + 1, d)
                    for d in range(1, m)
                ]
                self.d = y_copy(self.pd, dst.at[half(pb, yi)], base + 1)

            def run_a(self):
                self.a.start()

            def run_b(self):
                self.a.wait()
                both = self.own[half(self.pb, yi), :].astype(F32) + self.box[...].astype(F32)
                self.pair[...] = both.astype(BF)
                for copy in self.b:
                    copy.start()
                self.zbox[zi] = self.pair[z_of(zi), :]

            def run_c(self):
                wait(self.b)
                total = jnp.zeros((zrows, HD), F32)
                for s in self.order:
                    self.px[s] = total.astype(BF)
                    total = total + self.zbox[s].astype(F32)
                for copy in self.c:
                    copy.start()
                self.pz[z_of(zi), :] = self.px[zi]

            def run_d(self):
                wait(self.c)
                late = (yi if self.forward else yo).astype(F32)
                mine = half(self.pb, yi)
                base = self.pz[...].astype(F32)
                give = base + (1.0 - late) * self.own[mine, :].astype(F32)
                self.pd[...] = give.astype(BF)
                self.d.start()
                keep = base + late * self.box[...].astype(F32)
                self.dst[mine, :] = keep.astype(BF)

        order_f = (xp, diag, sib, me)
        order_b = (me, sib, xp, diag)
        bufs_f = (box1, pair1, zbox1, px1, pz1, pd1)
        bufs_b = (box2, pair2, zbox2, px2, pz2, pd2)
        fwd = [Scan(st, sb, bufs_f, g, pb, 2 * g, True) for g, pb in enumerate(order_f)]
        bwd = [Scan(rv, sa, bufs_b, g, pb, 2 * (np_ + g), False) for g, pb in enumerate(order_b)]

        for step, pb in enumerate(order_f):
            for i in range(per):
                ls = lanes(pb, i)
                st[ls, :] = dot(k[:, ls] * live_h, v[:, ls], 0, 0).astype(BF)
            fwd[step].run_a()

        row_i = lax.broadcasted_iota(jnp.int32, (rows, rows), 0)
        col_i = lax.broadcasted_iota(jnp.int32, (rows, rows), 1)
        rb, cb = row_i // (rows // nb), col_i // (rows // nb)
        keep = jnp.where(rb == cb, 1.0, 0.0).astype(F32)
        for i in range(nb):
            for j in range(i):
                on = jnp.where(vm[0, 0, i, j] == 1, 1.0, 0.0).astype(F32)
                keep = keep + jnp.where((rb == i) & (cb == j), on, 0.0)
        allowed[...] = jnp.where(row_i >= col_i, keep, 0.0) * live * live_r

        def scores(pb):
            for i in range(per):
                ls = lanes(pb, i)
                s = dot(q[:, ls], k[:, ls], 1, 1) * allowed[...]
                sc[pb * per + i] = s.astype(BF)

        def grad_block(pb):
            @pl.loop(0, blk // 256)
            def _(c):
                at = pl.ds(pl.multiple_of(c * 256, 256), 256)
                ga = dot(go[...], w_all[pb, at, :], 1, 1).astype(BF)
                gg = (scale * ga.astype(F32)).astype(BF)
                g[:, pl.ds(pl.multiple_of(pb * blk + c * 256, HD), 256)] = gg
                for i in range(256 // HD):
                    ls = pl.ds(pl.multiple_of(pb * blk + c * 256 + i * HD, HD), HD)
                    rv[ls, :] = dot(q[:, ls], gg[:, i * HD : (i + 1) * HD], 0, 0).astype(BF)

        def attend(pb):
            for i in range(per):
                ls = lanes(pb, i)
                inner = dot(sc[pb * per + i], v[:, ls], 1, 0) + dot(q[:, ls], sb[ls, :], 1, 0)
                att[pb, :, i * HD : (i + 1) * HD] = (scale * inner).astype(BF)

        def grads(pb):
            for i in range(per):
                ls = lanes(pb, i)
                gh = g[:, ls]
                inner = (dot(gh, v[:, ls], 1, 1) * allowed[...]).astype(BF)
                dq[:, ls] = (dot(inner, k[:, ls], 1, 0) + dot(gh, sb[ls, :], 1, 1)).astype(BF)
                dk0[:, ls] = dot(inner, q[:, ls], 0, 0)
                dv0[:, ls] = dot(sc[pb * per + i], gh, 0, 0)

        def finish(pb):
            for i in range(per):
                ls = lanes(pb, i)
                dk[:, ls] = (dk0[:, ls] + live * dot(v[:, ls], sa[ls, :], 1, 1)).astype(BF)
                dv[:, ls] = (dv0[:, ls] + live * dot(k[:, ls], sa[ls, :], 1, 0)).astype(BF)

        def product(cols):
            acc = dot(att_t[0], go_all[0, :, cols], 1, 0)
            for b in range(1, np_):
                acc = acc + dot(att_t[b], go_all[b, :, cols], 1, 0)
            return acc

        def cols_of(i):
            return pl.ds(pl.multiple_of(i * piece, HD), piece)

        def to_of(d):
            return (zi + d + 1) % m

        y_out = [y_copy(part.at[to_of(d) * 2 + yo], pbox.at[to_of(d)], n_scan_y + 3 + d) for d in range(m)]
        z_out = [z_copy(psum.at[to_of(d)], zpart.at[zi], 4 * np_, d + 1) for d in range(m - 1)]

        def y_part(d):
            to = to_of(d)
            if n_go > 1:
                part[to * 2 + yo] = product(cols_of(to * 2 + yo)).astype(BF)
            y_out[d].start()

        def z_part(d):
            to = to_of(d)
            if n_go > 1:
                acc = product(cols_of(to * 2 + yi))
            else:
                acc = part[to * 2 + yi].astype(F32)
            y_out[d].wait()
            acc = acc + pbox[to].astype(F32)
            psum[to] = acc.astype(BF)
            if d < m - 1:
                z_out[d].start()
            else:
                zpart[zi] = psum[to]

        def got_go(d):
            go_x[d].wait()
            go_relay[d].start()

        for i, pb in enumerate(order_f):
            scores(pb)
            fwd[i].run_b()
        local_w.wait()
        w_x[0].wait()
        w_z[0].start()
        w_y[0].start()
        w_relay[0].start()
        grad_block(me)
        bwd[0].run_a()
        fwd[0].run_c()
        fwd[1].run_c()
        w_sib.wait()
        grad_block(sib)
        bwd[1].run_a()
        fwd[2].run_c()
        fwd[3].run_c()
        w_x[1].wait()
        w_y[1].start()
        w_z[1].start()
        w_relay[1].start()
        for i in range(np_):
            fwd[i].run_d()
        bwd[0].run_b()
        bwd[1].run_b()
        w_z[0].wait()
        w_y[2].start()
        w_relay[2].start()
        if n_go > 1:
            go_x[1].start()
        for i, pb in enumerate(order_f):
            fwd[i].d.wait()
            attend(pb)
            if i < 3:
                att_out[i].start()
            if i == 1:
                for d in range(2, n_go):
                    go_x[d].start()
        bwd[0].run_c()
        bwd[1].run_c()
        w_y[1].wait()
        w_z[2].start()
        w_relay[5].start()
        w_y[0].wait()
        w_relay[4].start()
        grads(me)
        w_z[1].wait()
        w_relay[3].start()
        bwd[0].run_d()
        bwd[1].run_d()
        got_go(0)
        att_t[me] = att[me].T
        local_go.wait()
        go_sib.wait()
        w_y[2].wait()
        w_relay[6].start()
        grads(sib)
        w_z[2].wait()
        w_relay[7].start()
        grad_block(xp)
        bwd[2].run_a()
        wait(w_relay)
        grad_block(diag)
        bwd[3].run_a()
        for copy, peer in zip(att_out, (xp, diag, sib)):
            copy.wait()
            att_t[peer] = attc[peer].T
        go_relay[0].wait()
        if n_go == 1:
            for j in range(width // 256):
                acc = product(slice(j * 256, (j + 1) * 256))
                for i in range(256 // piece):
                    part[j * (256 // piece) + i] = acc[:, i * piece : (i + 1) * piece].astype(BF)
            for d in range(m):
                y_part(d)
            bwd[2].run_b()
            bwd[3].run_b()
            grads(xp)
            bwd[2].run_c()
            bwd[3].run_c()
            grads(diag)
            for d in range(m):
                z_part(d)
        else:
            y_part(0)
            bwd[2].run_b()
            grads(xp)
            bwd[3].run_b()
            got_go(1)
            go_relay[1].wait()
            y_part(1)
            bwd[2].run_c()
            z_part(0)
            grads(diag)
            bwd[3].run_c()
            for d in range(2, m):
                got_go(d)
                go_relay[d].wait()
                y_part(d)
                z_part(d - 1)
        bwd[2].run_d()
        bwd[3].run_d()
        if n_go > 1:
            z_part(m - 1)

        @pl.loop(0, width // 256)
        def _(j):
            cols = pl.ds(pl.multiple_of(j * 256, 256), 256)
            acc = dot(att[0], w_all[0, :, cols], 1, 0)
            for b in range(1, np_):
                acc = acc + dot(att[b], w_all[b, :, cols], 1, 0)
            mixed[:, cols] = acc.astype(BF)

        for i, pb in enumerate(order_b):
            bwd[i].d.wait()
            finish(pb)
        wait(z_out)
        total = zpart[0].astype(F32)
        for s in range(1, m):
            total = total + zpart[s].astype(F32)
        wg[...] = total * grad_scale

    vmem = pltpu.VMEM
    sems = pltpu.SemaphoreType.DMA
    state = vmem((heads * HD, HD), BF)
    half_state = vmem((np_, half_rows, HD), BF)
    by_z = vmem((np_, m, zrows, HD), BF)
    scan_boxes = [half_state, half_state, by_z, by_z, half_state, half_state]
    n_pat = 15 + 2 * n_go
    n_y = n_scan_y + 3 + m
    scratch = [
        vmem((np_, blk, width), BF),
        vmem((np_, rows, width), BF),
        vmem((np_, rows, blk), BF),
        vmem((np_, rows, blk), BF),
        vmem((np_, blk, rows), BF),
        vmem((heads, rows, rows), BF),
        vmem((rows, rows), F32),
        vmem((rows, width), BF),
        vmem((rows, width), F32),
        vmem((rows, width), F32),
        state, state, state, state,
        *scan_boxes,
        *scan_boxes,
        vmem((n, blk, piece), BF),
        vmem((m, blk, piece), BF),
        vmem((m, blk, piece), BF),
        vmem((m, blk, piece), BF),
        sems((8,)),
        sems((n_pat,)), sems((n_pat,)),
        sems((n_y,)), sems((n_y,)),
        sems((4 * np_ + 1, m)), sems((4 * np_ + 1, m)),
    ]
    full = jax.ShapeDtypeStruct((rows, width), BF)
    whole = pl.BlockSpec(memory_space=pltpu.VMEM)
    scalar = pl.BlockSpec(memory_space=pltpu.SMEM)
    return pl.pallas_call(
        kernel,
        out_shape=(full, full, full, full, jax.ShapeDtypeStruct((blk, piece), F32)),
        in_specs=[whole] * 5 + [scalar] * 2,
        out_specs=(whole,) * 5,
        scratch_shapes=scratch,
        compiler_params=pltpu.CompilerParams(
            collective_id=0, has_side_effects=True, vmem_limit_bytes=60 * 1024 * 1024
        ),
    )


def solution(mesh):
    n, np_ = mesh.shape["seq"], mesh.shape["pat"]

    def on_device(queries, key_rows, value_rows, out_weight, grad_out, visit_mask, lengths):
        rows, width = queries.shape[1:]
        call = make_kernel(
            n, np_, rows, width, visit_mask.shape[-1], 1.0 / math.sqrt(np_ * n * rows)
        )
        mixed, dq, dk, dv, wg = call(
            queries[0], key_rows[0], value_rows[0], grad_out[0], out_weight, visit_mask, lengths
        )
        return mixed[None], dq[None], dk[None], dv[None], wg

    rows3 = P("pat", "seq", None)
    return jax.shard_map(
        on_device,
        mesh=mesh,
        in_specs=(rows3, rows3, rows3, P("pat", None), rows3, P("pat", "seq", None, None), P("pat")),
        out_specs=(rows3, rows3, rows3, rows3, P("pat", "seq")),
        check_vma=False,
    )
```

time: 108 us -> 94.5 us (0.88)
  Pallas kernels: 100 us -> 86.2 us
    pallas_call x1, Pallas kernels: 100 us -> 86.2 us  [on_device(): call(queries[0], key_rows[0], value_rows[0], grad_out[0], out_weight, vis...]
where the time goes in v1:
time: 94.5 us; the launch traced here: 93.7 us
  Pallas kernels  86.2 us (91%)
  local copies, waits for them, and re-layouts  6.17 us (7%)
  between operations  1.31 us (1%)
    pallas_call x1, Pallas kernels, on_device(): call(queries[0], key_rows[0], value_rows[0], grad_out[0], out_weight, vis...  86.2 us
    unnamed x13, local copies, waits for them, and re-layouts  6.17 us

profile of v1, /device:TPU:24, one launch (start us, length us, event | category | flops | bytes accessed | tf_op | source)
XLA Modules:
  0.0 93.7 jit_solution(9719014882713996380)
XLA Ops:
  1.3 86.2 %shard_map.110 = (bf16[256,2048]{1,0:T(8,128)(2,1)}, bf16[256,2048]{1,0:T(8,128)(2,1)}, bf16[256,2048]{1,0:T(8,128)(2,1)}, bf16[256,2048]{1,0:T(8,128)(2,1)}, f32[512,256]{1,0:T(8,128)}) custom-call(bf16[256,2048]{1,0:T(8,128)(2,1)} %bitcast.12, bf16[256,2048]{1,0:T(8,128)(2,1)} %bitcast.13, bf16[256,2048]{1,0:T(8,128)(2,1)} %bitcast.14, ...), custom_call_target="tpu_custom_call" | custom-call | tf_op jit(solution)/shard_map/pallas_call | solution.py:476
  87.5 0.0 copy-start.2
  87.5 0.0 copy-start.1
  87.5 2.5 %copy.18 = bf16[1,256,2048]{2,1,0:T(8,128)(2,1)} copy(bf16[1,256,2048]{2,1,0:T(8,128)(2,1)} %bitcast.11) | data formatting | bytes 2097152
  90.0 0.0 copy-done.2
  90.0 0.0 copy-start
  90.0 1.0 %copy.19 = bf16[1,256,2048]{2,1,0:T(8,128)(2,1)} copy(bf16[1,256,2048]{2,1,0:T(8,128)(2,1)S(1)} %bitcast.10) | data formatting | bytes 2097152
  90.9 0.0 copy-done.1
  90.9 0.0 copy-start.3
  90.9 1.0 %copy.20 = bf16[1,256,2048]{2,1,0:T(8,128)(2,1)} copy(bf16[1,256,2048]{2,1,0:T(8,128)(2,1)S(1)} %bitcast.9) | data formatting | bytes 2097152
  91.9 0.0 copy-done
  91.9 1.0 %copy.21 = bf16[1,256,2048]{2,1,0:T(8,128)(2,1)} copy(bf16[1,256,2048]{2,1,0:T(8,128)(2,1)S(1)} %bitcast.8) | data formatting | bytes 2097152
  92.9 0.0 copy-done.3
  92.9 0.8 copy.22
Async XLA Ops:
  87.5 2.5 %copy-start.2 = (bf16[256,2048]{1,0:T(8,128)(2,1)S(1)}, bf16[256,2048]{1,0:T(8,128)(2,1)}, u32[]{:S(2)}) copy-start(bf16[256,2048]{1,0:T(8,128)(2,1)} %get-tuple-element.11) | copy-start | bytes 3145732
  87.5 3.4 %copy-start.1 = (bf16[256,2048]{1,0:T(8,128)(2,1)S(1)}, bf16[256,2048]{1,0:T(8,128)(2,1)}, u32[]{:S(2)}) copy-start(bf16[256,2048]{1,0:T(8,128)(2,1)} %get-tuple-element.12) | copy-start | bytes 3145732
  90.0 1.9 %copy-start = (bf16[256,2048]{1,0:T(8,128)(2,1)S(1)}, bf16[256,2048]{1,0:T(8,128)(2,1)}, u32[]{:S(2)}) copy-start(bf16[256,2048]{1,0:T(8,128)(2,1)} %get-tuple-element.13) | copy-start | bytes 3145732
  90.9 1.9 %copy-start.3 = (f32[512,256]{1,0:T(8,128)S(1)}, f32[512,256]{1,0:T(8,128)}, u32[]{:S(2)}) copy-start(f32[512,256]{1,0:T(8,128)} %get-tuple-element.24) | copy-start | bytes 1572868
